TPU v7x, 32 devices: a whole 2x2x4 slice. The times are simulated.
32 devices in a mesh: fsdp: 8 (over z, x), tensor: 4 (over y, core).
Axes of the slice: x: 2, y: 2, z: 4, core: 2. Of those that a mesh axis runs over, the one named last changes fastest.
Arguments:
- inputs: bfloat16 [16384, 1024], P(('fsdp', 'tensor')), may hold values from -6 to 6
- segments: int32 [16384], P('fsdp'), may hold values from 0 to 303, as said below
- cotangent: bfloat16 [16384, 1024], P(('fsdp', 'tensor')), may hold values from -6 to 6
- attention_gain: float32 [1024], P(('fsdp', 'tensor')), may hold values from 0.5 to 1.5
- attention_shift: float32 [1024], P(('fsdp', 'tensor')), may hold values from -1.8 to 1.8
- feedforward_gain: float32 [1024], P(('fsdp', 'tensor')), may hold values from 0.5 to 1.5
- feedforward_shift: float32 [1024], P(('fsdp', 'tensor')), may hold values from -1.8 to 1.8
- project_weight: bfloat16 [1024, 3072], P('fsdp', 'tensor'), may hold values from -0.1875 to 0.1875
- project_bias: bfloat16 [3072], P(('tensor', 'fsdp')), may hold values from -3 to 3
- dense_weight: bfloat16 [1024, 1024], P(('tensor', 'fsdp')), may hold values from -0.75 to 0.75
- dense_bias: float32 [1024], P(('fsdp', 'tensor')), may hold values from -1.8 to 1.8
- expand_weight: bfloat16 [1024, 4096], P('fsdp', 'tensor'), may hold values from -0.1875 to 0.1875
- expand_bias: bfloat16 [4096], P(('tensor', 'fsdp')), may hold values from -3 to 3
- shrink_weight: bfloat16 [4096, 1024], P(('tensor', 'fsdp')), may hold values from -0.09375 to 0.09375
- shrink_bias: float32 [1024], P(('fsdp', 'tensor')), may hold values from -1.8 to 1.8
Outputs:
- output: bfloat16 [16384, 1024], P(('fsdp', 'tensor'))
- inputs_gradient: bfloat16 [16384, 1024], P(('fsdp', 'tensor'))
- attention_gain_gradient: float32 [1024], P(('fsdp', 'tensor'))
- attention_shift_gradient: float32 [1024], P(('fsdp', 'tensor'))
- feedforward_gain_gradient: float32 [1024], P(('fsdp', 'tensor'))
- feedforward_shift_gradient: float32 [1024], P(('fsdp', 'tensor'))
- project_weight_gradient: float32 [1024, 3072], P('fsdp', 'tensor')
- project_bias_gradient: float32 [3072], P(('tensor', 'fsdp'))
- dense_weight_gradient: float32 [1024, 1024], P(('tensor', 'fsdp'))
- dense_bias_gradient: float32 [1024], P(('fsdp', 'tensor'))
- expand_weight_gradient: float32 [1024, 4096], P('fsdp', 'tensor')
- expand_bias_gradient: float32 [4096], P(('tensor', 'fsdp'))
- shrink_weight_gradient: float32 [4096, 1024], P(('tensor', 'fsdp'))
- shrink_bias_gradient: float32 [1024], P(('fsdp', 'tensor'))
Inputs may be any that keep to these rules, and one draw needn't show every extreme that they name: `segments`: within each aligned run of 1024 tokens (one sequence) the nonzero segment numbers never fall and occur in no other run; 0 marks padding, which stands only at the end of a run.
All inputs are finite; a program needn't handle non-finite values.
Results may differ from a plain program's by a relative error of at most 0.012.
Values may be sent and summed in bfloat16 or wider, within the bound.
No kernel may reach another device: no remote copies, remote signals or barrier semaphores. Data moves between devices by JAX's collectives and lax.ppermute only.
A program may use at most 192 MiB of HBM per device.

v0:
```python
from functools import partial
import math
import jax
import jax.numpy as jnp
from jax import lax
from jax.sharding import PartitionSpec as P

HD = 64
ROT = 16
SEQ_LEN = 1024
EPS = 1e-05
NEGATIVE = -1e30


def layer_norm(values, gain, shift):
    centre = values - jnp.mean(values, axis=-1, keepdims=True)
    spread = jnp.mean(centre * centre, axis=-1, keepdims=True)
    return centre * lax.rsqrt(spread + EPS) * gain + shift


def rotary_tables(positions):
    half = ROT // 2
    rates = jnp.exp(
        jnp.arange(half, dtype=jnp.int32).astype(jnp.float32) * (-2.0 * math.log(10000.0) / ROT)
    )
    angles = positions.astype(jnp.float32)[:, None] * rates[None, :]
    cosine = jnp.concatenate([jnp.cos(angles), jnp.cos(angles)], axis=1)[:, None, :]
    sine = jnp.concatenate([jnp.sin(angles), jnp.sin(angles)], axis=1)[:, None, :]
    return (cosine, sine)


def rotate(vectors, cosine, sine):
    half = ROT // 2
    turned = vectors[..., :ROT]
    swapped = jnp.concatenate([-turned[..., half:], turned[..., :half]], axis=-1)
    return jnp.concatenate([turned * cosine + swapped * sine, vectors[..., ROT:]], axis=-1)


def rotate_back(grads, cosine, sine):
    half = ROT // 2
    turned = grads[..., :ROT]
    scaled = turned * sine
    backward = jnp.concatenate([scaled[..., half:], -scaled[..., :half]], axis=-1)
    return jnp.concatenate([turned * cosine + backward, grads[..., ROT:]], axis=-1)


def allowed_mask(query_labels, key_labels, query_start):
    query_index = query_start + jnp.arange(query_labels.shape[0], dtype=jnp.int32)
    key_index = jnp.arange(key_labels.shape[0], dtype=jnp.int32)
    causal = key_index[None, :] <= query_index[:, None]
    same = query_labels[:, None] == key_labels[None, :]
    alone = (query_labels[:, None] != 0) | (key_index[None, :] == query_index[:, None])
    return causal & same & alone


def block_scores(query_block, keys, labels, start):
    scale = 1.0 / math.sqrt(HD)
    scores = (
        jnp.einsum("qhd,khd->hqk", query_block, keys, preferred_element_type=jnp.float32) * scale
    )
    mask = allowed_mask(labels[start : start + query_block.shape[0]], labels, start)
    return jnp.where(mask[None], scores, NEGATIVE)


def attend_sequence(items):
    query, keys, values, labels = items
    length = keys.shape[0]
    rows_block = min(512, length)
    outputs = []
    totals = []
    for block in range(length // rows_block):
        start = block * rows_block
        scores = block_scores(query[start : start + rows_block], keys, labels, start)
        top = jnp.max(scores, axis=-1, keepdims=True)
        probs = jnp.exp(scores - top)
        total = jnp.sum(probs, axis=-1, keepdims=True)
        probs = probs / total
        mixed = jnp.einsum(
            "hqk,khd->qhd", probs.astype(jnp.bfloat16), values, preferred_element_type=jnp.float32
        )
        outputs.append(mixed.astype(jnp.bfloat16))
        totals.append((top + jnp.log(total))[..., 0])
    return (jnp.concatenate(outputs, axis=0), jnp.concatenate(totals, axis=1))


def attend_back(items):
    query, keys, values, labels, totals, grads = items
    scale = 1.0 / math.sqrt(HD)
    length = keys.shape[0]
    rows_block = min(512, length)
    key_grad = jnp.zeros(keys.shape, jnp.float32)
    value_grad = jnp.zeros(values.shape, jnp.float32)
    query_grads = []
    for block in range(length // rows_block):
        start = block * rows_block
        query_block = query[start : start + rows_block]
        grad_block = grads[start : start + rows_block]
        scores = block_scores(query_block, keys, labels, start)
        probs = jnp.exp(scores - totals[:, start : start + rows_block, None])
        probs_grad = jnp.einsum(
            "qhd,khd->hqk", grad_block, values, preferred_element_type=jnp.float32
        )
        inner = jnp.sum(probs * probs_grad, axis=-1, keepdims=True)
        scores_grad = (probs * (probs_grad - inner)).astype(jnp.bfloat16)
        query_grads.append(
            jnp.einsum("hqk,khd->qhd", scores_grad, keys, preferred_element_type=jnp.float32)
            * scale
        )
        key_grad = (
            key_grad
            + jnp.einsum(
                "hqk,qhd->khd", scores_grad, query_block, preferred_element_type=jnp.float32
            )
            * scale
        )
        value_grad = value_grad + jnp.einsum(
            "hqk,qhd->khd",
            probs.astype(jnp.bfloat16),
            grad_block,
            preferred_element_type=jnp.float32,
        )
    return (jnp.concatenate(query_grads, axis=0), key_grad, value_grad)


def contract_rows(left, right):
    return lax.dot_general(
        left, right, (((0,), (0,)), ((), ())), preferred_element_type=jnp.float32
    )


def contract_columns(left, right):
    return lax.dot_general(
        left, right, (((1,), (1,)), ((), ())), preferred_element_type=jnp.float32
    )


def local(
    inputs,
    segments,
    cotangent,
    attention_gain,
    attention_shift,
    feedforward_gain,
    feedforward_shift,
    project_weight,
    project_bias,
    dense_weight,
    dense_bias,
    expand_weight,
    expand_bias,
    shrink_weight,
    shrink_bias,
):
    rank = lax.axis_index("tensor")
    rows = inputs.shape[0]
    group = segments.shape[0]
    count = group // SEQ_LEN
    vectors = (
        lax.all_gather(attention_gain, ("fsdp", "tensor"), axis=0, tiled=True),
        lax.all_gather(attention_shift, ("fsdp", "tensor"), axis=0, tiled=True),
        lax.all_gather(feedforward_gain, ("fsdp", "tensor"), axis=0, tiled=True),
        lax.all_gather(feedforward_shift, ("fsdp", "tensor"), axis=0, tiled=True),
        lax.all_gather(dense_bias, ("fsdp", "tensor"), axis=0, tiled=True),
        lax.all_gather(shrink_bias, ("fsdp", "tensor"), axis=0, tiled=True),
    )
    gain_one, shift_one, gain_two, shift_two, dense_full, shrink_full = vectors
    gathered = (
        lax.all_gather(project_weight, "fsdp", axis=0, tiled=True),
        lax.all_gather(expand_weight, "fsdp", axis=0, tiled=True),
        lax.all_gather(dense_weight, "fsdp", axis=0, tiled=True),
        lax.all_gather(shrink_weight, "fsdp", axis=0, tiled=True),
        lax.all_gather(project_bias, "fsdp", axis=0, tiled=True),
        lax.all_gather(expand_bias, "fsdp", axis=0, tiled=True),
    )
    project_local, expand_local, dense_local, shrink_local, project_offset, expand_offset = gathered
    features = inputs.astype(jnp.float32)
    local_one = layer_norm(features, gain_one, shift_one).astype(jnp.bfloat16)
    local_two = layer_norm(features, gain_two, shift_two).astype(jnp.bfloat16)
    normed_one, normed_two = (
        lax.all_gather(local_one, "tensor", axis=0, tiled=True),
        lax.all_gather(local_two, "tensor", axis=0, tiled=True),
    )
    positions = jnp.arange(group, dtype=jnp.int32) % SEQ_LEN
    cosine, sine = rotary_tables(positions)
    heads = project_local.shape[1] // (3 * HD)
    projected = jnp.dot(
        normed_one, project_local, preferred_element_type=jnp.float32
    ) + project_offset.astype(jnp.float32)
    projected = projected.reshape(group, heads, 3, HD)
    query = rotate(projected[:, :, 0], cosine, sine).astype(jnp.bfloat16)
    keys = rotate(projected[:, :, 1], cosine, sine).astype(jnp.bfloat16)
    values = projected[:, :, 2].astype(jnp.bfloat16)

    def shaped(array):
        return array.reshape((count, SEQ_LEN) + array.shape[1:])

    labels = segments.reshape(count, SEQ_LEN)
    mixed, totals = lax.map(attend_sequence, (shaped(query), shaped(keys), shaped(values), labels))
    mixed = mixed.reshape(group, heads * HD)
    hidden = jnp.dot(
        normed_two, expand_local, preferred_element_type=jnp.float32
    ) + expand_offset.astype(jnp.float32)
    active = jax.nn.gelu(hidden, approximate=False).astype(jnp.bfloat16)
    mixed_rows = lax.slice_in_dim(mixed, 0, rows * lax.axis_size("tensor"), axis=0)
    branch = lax.psum_scatter(
        (
            jnp.dot(mixed_rows, dense_local, preferred_element_type=jnp.float32)
            + jnp.dot(active, shrink_local, preferred_element_type=jnp.float32)
        ).astype(jnp.bfloat16),
        "tensor",
        scatter_dimension=0,
        tiled=True,
    ).astype(jnp.float32)
    output = (features + branch + dense_full + shrink_full).astype(jnp.bfloat16)
    own_labels = lax.dynamic_slice_in_dim(segments, rank * rows, rows, 0)
    upstream = cotangent.astype(jnp.float32) * (own_labels != 0).astype(jnp.float32)[:, None]
    branch_grad = lax.all_gather(upstream.astype(jnp.bfloat16), "tensor", axis=0, tiled=True)
    bias_grad = jnp.sum(upstream, axis=0)
    shrink_grad = contract_rows(active, branch_grad)
    active_grad = contract_columns(branch_grad, shrink_local)
    gelu_value, gelu_pull = jax.vjp(partial(jax.nn.gelu, approximate=False), hidden)
    hidden_grad = gelu_pull(active_grad)[0].astype(jnp.bfloat16)
    expand_grad = contract_rows(normed_two, hidden_grad)
    expand_offset_grad = jnp.sum(hidden_grad.astype(jnp.float32), axis=0)
    normed_two_grad = contract_columns(hidden_grad, expand_local)
    dense_grad = contract_rows(mixed, branch_grad)
    mixed_grad = (
        contract_columns(branch_grad, dense_local).astype(jnp.bfloat16).reshape(group, heads, HD)
    )
    query_grad, key_grad, value_grad = lax.map(
        attend_back,
        (shaped(query), shaped(keys), shaped(values), labels, totals, shaped(mixed_grad)),
    )
    query_grad = rotate_back(query_grad.reshape(group, heads, HD), cosine, sine)
    key_grad = rotate_back(key_grad.reshape(group, heads, HD), cosine, sine)
    projected_grad = jnp.stack([query_grad, key_grad, value_grad.reshape(group, heads, HD)], axis=2)
    projected_grad = projected_grad.reshape(group, 3 * heads * HD).astype(jnp.bfloat16)
    project_grad = contract_rows(normed_one, projected_grad)
    project_offset_grad = jnp.sum(projected_grad.astype(jnp.float32), axis=0)
    normed_one_grad = contract_columns(projected_grad, project_local)
    weight_sums = (
        lax.psum_scatter(project_grad, "fsdp", scatter_dimension=0, tiled=True),
        lax.psum_scatter(expand_grad, "fsdp", scatter_dimension=0, tiled=True),
        lax.psum_scatter(dense_grad, "fsdp", scatter_dimension=0, tiled=True),
        lax.psum_scatter(shrink_grad, "fsdp", scatter_dimension=0, tiled=True),
        lax.psum_scatter(project_offset_grad, "fsdp", scatter_dimension=0, tiled=True),
        lax.psum_scatter(expand_offset_grad, "fsdp", scatter_dimension=0, tiled=True),
    )
    project_sum, expand_sum, dense_sum, shrink_sum, project_offset_sum, expand_offset_sum = (
        weight_sums
    )
    one_rows, two_rows = (
        lax.psum_scatter(
            normed_one_grad.astype(jnp.bfloat16), "tensor", scatter_dimension=0, tiled=True
        ).astype(jnp.float32),
        lax.psum_scatter(
            normed_two_grad.astype(jnp.bfloat16), "tensor", scatter_dimension=0, tiled=True
        ).astype(jnp.float32),
    )
    norm_value, first_pull = jax.vjp(layer_norm, features, gain_one, shift_one)
    first_inputs, first_gain, first_shift = first_pull(one_rows)
    norm_other, second_pull = jax.vjp(layer_norm, features, gain_two, shift_two)
    second_inputs, second_gain, second_shift = second_pull(two_rows)
    inputs_gradient = (upstream + first_inputs + second_inputs).astype(jnp.bfloat16)
    vector_sums = (
        lax.psum_scatter(first_gain, ("fsdp", "tensor"), scatter_dimension=0, tiled=True),
        lax.psum_scatter(first_shift, ("fsdp", "tensor"), scatter_dimension=0, tiled=True),
        lax.psum_scatter(second_gain, ("fsdp", "tensor"), scatter_dimension=0, tiled=True),
        lax.psum_scatter(second_shift, ("fsdp", "tensor"), scatter_dimension=0, tiled=True),
        lax.psum_scatter(bias_grad, ("fsdp", "tensor"), scatter_dimension=0, tiled=True),
    )
    gain_one_sum, shift_one_sum, gain_two_sum, shift_two_sum, bias_sum = vector_sums
    return (
        output,
        inputs_gradient,
        gain_one_sum,
        shift_one_sum,
        gain_two_sum,
        shift_two_sum,
        project_sum,
        project_offset_sum,
        dense_sum,
        bias_sum,
        expand_sum,
        expand_offset_sum,
        shrink_sum,
        bias_sum,
    )


def solution(mesh):
    in_specs = (
        P(("fsdp", "tensor"), None),
        P("fsdp"),
        P(("fsdp", "tensor"), None),
        P(("fsdp", "tensor")),
        P(("fsdp", "tensor")),
        P(("fsdp", "tensor")),
        P(("fsdp", "tensor")),
        P("fsdp", "tensor"),
        P(("tensor", "fsdp")),
        P(("tensor", "fsdp"), None),
        P(("fsdp", "tensor")),
        P("fsdp", "tensor"),
        P(("tensor", "fsdp")),
        P(("tensor", "fsdp"), None),
        P(("fsdp", "tensor")),
    )
    out_specs = (
        P(("fsdp", "tensor"), None),
        P(("fsdp", "tensor"), None),
        P(("fsdp", "tensor")),
        P(("fsdp", "tensor")),
        P(("fsdp", "tensor")),
        P(("fsdp", "tensor")),
        P("fsdp", "tensor"),
        P(("tensor", "fsdp")),
        P(("tensor", "fsdp"), None),
        P(("fsdp", "tensor")),
        P("fsdp", "tensor"),
        P(("tensor", "fsdp")),
        P(("tensor", "fsdp"), None),
        P(("fsdp", "tensor")),
    )
    return jax.shard_map(local, mesh=mesh, in_specs=in_specs, out_specs=out_specs, check_vma=False)
```

profile of v0, /device:TPU:0, one launch (start us, length us, event | category | flops | bytes accessed | tf_op | source)
XLA Modules:
  0.0 900.5 jit_solution(8306996030455223238)
XLA Ops:
  11.4 42.7 %all-reduce.15 = (f32[1024]{0:T(1024)S(1)}, f32[1024]{0:T(1024)S(1)}, f32[1024]{0:T(1024)S(1)}, f32[1024]{0:T(1024)S(1)}) all-reduce(f32[1024]{0:T(1024)S(1)} %dynamic-update-slice.4, f32[1024]{0:T(1024)S(1)} %dynamic-update-slice.3, f32[1024]{0:T(1024)S(1)} %dynamic-update-slice.1, ...), channel_id=1, replica_groups=mesh['fsdp'=8,'tensor'=4] {'fsdp','tensor'}, use_global_device_ids=true, to_apply=%add.4 | all-reduce | flops 4096 | bytes 32768
  66.4 21.0 %all-reduce.2 = bf16[768]{0:T(1024)(128)(2,1)S(1)} all-reduce(bf16[768]{0:T(1024)(128)(2,1)S(1)} %dynamic-update-slice.2), channel_id=1, replica_groups=mesh['fsdp'=8,'tensor'=4] {'fsdp'}, use_global_device_ids=true, to_apply=%add.2 | all-reduce | flops 768 | bytes 3072
  87.3 33.6 %all_gather.50 = bf16[256,1024]{1,0:T(8,128)(2,1)} all-gather(bf16[32,1024]{1,0:T(8,128)(2,1)S(1)} %copy-done.28), channel_id=1, replica_groups=mesh['fsdp'=8,'tensor'=4] {'fsdp'}, dimensions={0}, use_global_device_ids=true | all-gather | bytes 589824 | tf_op jit(solution)/shard_map/all_gather | solution.py:170
  121.4 5.8 convolution_add_fusion.1
  142.6 37.2 %while.26 = (s32[]{:T(128)}, bf16[2,1024,4,64]{1,3,2,0:T(8,128)(2,1)}, f32[2,4,1024]{2,1,0:T(4,128)S(1)}, bf16[2,1024,4,64]{1,3,2,0:T(8,128)(2,1)}, s32[2,1024]{...) while((s32[]{:T(128)}, ...), condition=%wide.region_7.8_spmd, body=%wide.region_2.7_spmd.sunk | while | flops 1131677184 | bytes 58922628 | solution.py:198
  153.3 3.6 fusion.212
  156.9 3.6 fusion.209
  171.6 3.6 fusion.212
  175.3 3.6 fusion.209
  179.8 4.5 convolution_convert_fusion.2
  184.3 4.4 reshape.530
  188.7 4.1 copy.57
  192.9 193.4 %while.27 = (s32[]{:T(128)}, f32[2,1024,4,64]{1,0,3,2:T(2,128)}, f32[2,1024,4,64]{1,0,3,2:T(2,128)}, bf16[2,1024,4,64]{1,0,3,2:T(2,128)(2,1)}, bf16[2,1024,4,64]...) while((s32[]{:T(128)}, f32[2,1024,4,64]{1,0,3,2:T(2,128)}, ...), condition=%wide.region_12.13_spmd, body=%wide.region_9.12_spmd.sunk | while | flops 2755130880 | bytes 284876160 | solution.py:230
  196.5 4.6 multiply_reduce_fusion.5
  205.6 4.6 multiply_reduce_fusion.4
  215.8 18.7 %dynamic_update_slice.28 = f32[2,1024,4,64]{1,0,3,2:T(2,128)} dynamic-update-slice(f32[2,1024,4,64]{1,0,3,2:T(2,128)} %get-tuple-element.462, f32[1,1024,4,64]{1,0,3,2:T(1,128)S(1)} %copy.97, s32[]{:T(128)} %get-tuple-element.460, s32[]{:T(128)} %constant.44.clone.1..sunk.1, s32[]{:T(128)} %constant.44.clone.1..sunk.1, s32[]{:T(128)} %constant.44.clone.1..sunk.1) | dynamic-update-slice | bytes 2097156 | tf_op jit(solution)/shard_map/while/body/jit(dynamic_update_index_in_dim)/dynamic_update_slice | solution.py:230
  234.5 3.7 fusion.230
  240.8 18.7 %dynamic_update_slice.27 = f32[2,1024,4,64]{1,0,3,2:T(2,128)} dynamic-update-slice(f32[2,1024,4,64]{1,0,3,2:T(2,128)} %get-tuple-element.461, f32[1,1024,4,64]{1,0,3,2:T(1,128)S(1)} %copy.96, s32[]{:T(128)} %get-tuple-element.460, s32[]{:T(128)} %constant.44.clone.1..sunk.1, s32[]{:T(128)} %constant.44.clone.1..sunk.1, s32[]{:T(128)} %constant.44.clone.1..sunk.1) | dynamic-update-slice | bytes 2097156 | tf_op jit(solution)/shard_map/while/body/jit(dynamic_update_index_in_dim)/dynamic_update_slice | solution.py:230
  259.5 5.8 fusion.233
  265.3 5.9 fusion.234
  272.1 17.4 %dynamic_update_slice.29 = bf16[2,1024,4,64]{1,0,3,2:T(2,128)(2,1)} dynamic-update-slice(bf16[2,1024,4,64]{1,0,3,2:T(2,128)(2,1)} %get-tuple-element.463, bf16[1,1024,4,64]{1,0,3,2:T(2,128)(2,1)S(1)} %copy.98, s32[]{:T(128)} %get-tuple-element.460, s32[]{:T(128)} %constant.44.clone.1..sunk.1, s32[]{:T(128)} %constant.44.clone.1..sunk.1, s32[]{:T(128)} %constant.44.clone.1..sunk.1) | dynamic-update-slice | bytes 1048580 | tf_op jit(solution)/shard_map/while/body/jit(dynamic_update_index_in_dim)/dynamic_update_slice | solution.py:230
  292.9 4.6 multiply_reduce_fusion.5
  302.1 4.6 multiply_reduce_fusion.4
  312.3 18.7 %dynamic_update_slice.28 = f32[2,1024,4,64]{1,0,3,2:T(2,128)} dynamic-update-slice(f32[2,1024,4,64]{1,0,3,2:T(2,128)} %get-tuple-element.462, f32[1,1024,4,64]{1,0,3,2:T(1,128)S(1)} %copy.97, s32[]{:T(128)} %get-tuple-element.460, s32[]{:T(128)} %constant.44.clone.1..sunk.1, s32[]{:T(128)} %constant.44.clone.1..sunk.1, s32[]{:T(128)} %constant.44.clone.1..sunk.1) | dynamic-update-slice | bytes 2097156 | tf_op jit(solution)/shard_map/while/body/jit(dynamic_update_index_in_dim)/dynamic_update_slice | solution.py:230
  331.0 3.7 fusion.230
  337.3 18.7 %dynamic_update_slice.27 = f32[2,1024,4,64]{1,0,3,2:T(2,128)} dynamic-update-slice(f32[2,1024,4,64]{1,0,3,2:T(2,128)} %get-tuple-element.461, f32[1,1024,4,64]{1,0,3,2:T(1,128)S(1)} %copy.96, s32[]{:T(128)} %get-tuple-element.460, s32[]{:T(128)} %constant.44.clone.1..sunk.1, s32[]{:T(128)} %constant.44.clone.1..sunk.1, s32[]{:T(128)} %constant.44.clone.1..sunk.1) | dynamic-update-slice | bytes 2097156 | tf_op jit(solution)/shard_map/while/body/jit(dynamic_update_index_in_dim)/dynamic_update_slice | solution.py:230
  355.9 5.7 fusion.233
  361.7 5.9 fusion.234
  368.4 17.4 %dynamic_update_slice.29 = bf16[2,1024,4,64]{1,0,3,2:T(2,128)(2,1)} dynamic-update-slice(bf16[2,1024,4,64]{1,0,3,2:T(2,128)(2,1)} %get-tuple-element.463, bf16[1,1024,4,64]{1,0,3,2:T(2,128)(2,1)S(1)} %copy.98, s32[]{:T(128)} %get-tuple-element.460, s32[]{:T(128)} %constant.44.clone.1..sunk.1, s32[]{:T(128)} %constant.44.clone.1..sunk.1, s32[]{:T(128)} %constant.44.clone.1..sunk.1) | dynamic-update-slice | bytes 1048580 | tf_op jit(solution)/shard_map/while/body/jit(dynamic_update_index_in_dim)/dynamic_update_slice | solution.py:230
  389.3 4.0 reshape.509
  404.7 5.3 convolution_convert_fusion
  410.6 16.1 %all-gather = bf16[8,1,128]{2,1,0:T(2,128)(2,1)S(1)} all-gather(bf16[1,1,128]{2,1,0:T(2,128)(2,1)S(1)} %bitcast.260), channel_id=1, replica_groups=mesh['fsdp'=8,'tensor'=4] {'fsdp'}, dimensions={0}, use_global_device_ids=true | all-gather | bytes 2304 | tf_op jit(solution)/shard_map/all_gather | solution.py:173
  426.8 10.7 %fusion.139 = f32[2048,1024]{1,0:T(8,128)} fusion(bf16[2048,1024]{1,0:T(8,128)(2,1)} %all-gather.12.cloned.1.call-done, bf16[1024,1024]{1,0:T(8,128)(2,1)} %all-gather.14.cloned.1.call-done), kind=kOutput, calls=%fused_computation.245 | convolution fusion | flops 4294967296 | bytes 14680064 | tf_op jit(solution)/shard_map/dot_general | solution.py:200
  437.5 28.0 %convert_reduce_fusion = (f32[1024]{0:T(1024)S(1)}, bf16[2048,1024]{1,0:T(8,128)(2,1)S(1)}, f32[2048,1024]{1,0:T(8,128)}) fusion(f32[2048,1024]{1,0:T(8,128)} %fusion.139, f32[1024]{0:T(1024)S(1)} %bitcast.258, bf16[2048,1024]{1,0:T(8,128)(2,1)} %all-gather.18.cloned.1.call-done, bf16[1024,1024]{1,0:T(8,128)(2,1)} %all-gather.16.cloned.1.call-done), kind=kOutput, calls=%fused_computation.132 | convolution fusion | flops 4452252672 | bytes 27271168 | tf_op jit(solution)/shard_map/dot_general | solution.py:132
  467.4 6.4 convolution_convert_fusion.1
  476.7 12.3 %multiply_convert_fusion.2 = bf16[2048,1024]{1,0:T(8,128)(2,1)} fusion(f32[2048,1024]{1,0:T(8,128)} %get-tuple-element.214, f32[2048,1024]{1,0:T(8,128)} %fusion.139, f32[1024]{0:T(1024)S(1)} %bitcast.259), kind=kLoop, calls=%fused_computation.135 | loop fusion | flops 8388608 | bytes 20975616 | tf_op jit(solution)/shard_map/convert_element_type | solution.py:203
  489.0 6.4 fusion.140
  498.7 4.5 fusion.142
  503.3 8.4 fusion.141
  512.0 10.0 %fusion.144 = f32[1024,1024]{1,0:T(8,128)} fusion(bf16[2048,1024]{1,0:T(8,128)(2,1)} %multiply_convert_fusion.2, bf16[2048,1024]{1,0:T(8,128)(2,1)} %all-gather.18.cloned.1.call-done), kind=kOutput, calls=%fused_computation.250 | convolution fusion | flops 4294967296 | bytes 12582912 | tf_op jit(solution)/shard_map/dot_general | solution.py:126
  522.1 10.5 %fusion.143 = f32[1024,1024]{1,0:T(8,128)} fusion(bf16[2048,1024]{1,0:T(8,128)(2,1)} %all-gather.12.cloned.1.call-done, bf16[2048,1024]{1,0:T(8,128)(2,1)} %copy-done.46), kind=kOutput, calls=%fused_computation.249 | convolution fusion | flops 4294967296 | bytes 12582912 | tf_op jit(solution)/shard_map/dot_general | solution.py:126
  534.8 20.0 %all-reduce.16 = (f32[768]{0:T(1024)S(1)}, f32[1024]{0:T(1024)S(1)}) all-reduce(f32[768]{0:T(1024)S(1)} %reduce_sum.174, f32[1024]{0:T(1024)S(1)} %get-tuple-element.212), channel_id=10, replica_groups=mesh['fsdp'=8,'tensor'=4] {'fsdp'}, use_global_device_ids=true, to_apply=%region_29.30.clone | all-reduce | flops 1792 | bytes 14336
  558.6 3.4 fusion.118
  564.6 37.5 %all-reduce.14 = (f32[1024]{0:T(1024)S(1)}, f32[1024]{0:T(1024)S(1)}, f32[1024]{0:T(1024)S(1)}, f32[1024]{0:T(1024)S(1)}, f32[1024]{0:T(1024)S(1)}, /*index=5*/f32[1024]{0:T(1024)S(1)}, f32[1024]{0:T(1024)S(1)}) all-reduce(f32[1024]{0:T(1024)S(1)} %dynamic-update-slice.6, ...), channel_id=1, replica_groups=mesh['fsdp'=8,'tensor'=4] {'fsdp','tensor'}, use_global_device_ids=true, to_apply=%add.6 | all-reduce | flops 7168 | bytes 57344
  607.2 24.7 %reduce-scatter.16.cloned.1.call-done = f32[32,1024]{1,0:T(8,128)} async-done(((f32[256,1024]{1,0:T(8,128)}), f32[32,1024]{1,0:T(8,128)}) %reduce-scatter.16.cloned.1.call-update) | async-done | bytes 131088 | tf_op jit(solution)/shard_map/reduce_scatter | solution.py:244
  631.9 77.4 %reduce-scatter.14.cloned.1.call-done = f32[128,768]{1,0:T(8,128)} async-done(((f32[1024,768]{1,0:T(8,128)}), f32[128,768]{1,0:T(8,128)}) %reduce-scatter.14.cloned.1.call-update) | async-done | bytes 393232 | tf_op jit(solution)/shard_map/reduce_scatter | solution.py:242
  709.3 91.2 %reduce-scatter.20.cloned.1.call-done = f32[128,1024]{1,0:T(8,128)} async-done(((f32[1024,1024]{1,0:T(8,128)}), f32[128,1024]{1,0:T(8,128)}) %reduce-scatter.20.cloned.1.call-update) | async-done | bytes 524304 | tf_op jit(solution)/shard_map/reduce_scatter | solution.py:245
  800.5 92.5 %reduce-scatter.18.cloned.1.call-done = f32[128,1024]{1,0:T(8,128)} async-done(((f32[1024,1024]{1,0:T(8,128)}), f32[128,1024]{1,0:T(8,128)}) %reduce-scatter.18.cloned.1.call-update) | async-done | bytes 524304 | tf_op jit(solution)/shard_map/reduce_scatter | solution.py:243
  (291 shorter events, 123.1 us)
Async XLA Ops:
  7.2 53.9 %copy-start.36 = (s32[2048]{0:T(1024)S(1)}, s32[2048]{0:T(1024)}, u32[]{:S(2)}) copy-start(s32[2048]{0:T(1024)} %param.20) | copy-start | bytes 24580
  7.2 54.6 %copy-start.11 = (bf16[512,1024]{1,0:T(8,128)(2,1)S(1)}, bf16[512,1024]{1,0:T(8,128)(2,1)}, u32[]{:S(2)}) copy-start(bf16[512,1024]{1,0:T(8,128)(2,1)} %param.21) | copy-start | bytes 3145732
  7.2 114.1 %all-gather.10.cloned.1.call-start = ((), (), s32[]{:S(2)}) async-start(), calls=%async_computation.8 | async-start | bytes 1769472 | tf_op jit(solution)/shard_map/all_gather | solution.py:168
  7.9 113.4 %all-gather.8.cloned.1.call-start = ((), (), s32[]{:S(2)}) async-start(), calls=%async_computation.7 | async-start | bytes 5242880 | tf_op jit(solution)/shard_map/all_gather | solution.py:180
  54.1 8.9 copy-start.24
  54.1 8.9 copy-start.26
  57.2 3.8 copy-start.29
  57.8 7.1 copy-start.37
  57.8 8.4 copy-start.42
  57.8 29.6 %copy-start.28 = (bf16[32,1024]{1,0:T(8,128)(2,1)S(1)}, bf16[32,1024]{1,0:T(8,128)(2,1)}, u32[]{:S(2)}) copy-start(bf16[32,1024]{1,0:T(8,128)(2,1)} %param.28) | copy-start | bytes 196612
  61.0 118.8 %all-gather.18.cloned.1.call-start = ((), (), s32[]{:S(2)}) async-start(), calls=%async_computation.13 | async-start | bytes 5242880 | tf_op jit(solution)/shard_map/all_gather | solution.py:217
  63.0 363.8 %all-gather.14.cloned.1.call-start = ((), (), s32[]{:S(2)}) async-start(), calls=%async_computation.10 | async-start | bytes 2359296 | tf_op jit(solution)/shard_map/all_gather | solution.py:169
  63.6 363.2 %all-gather.12.cloned.1.call-start = ((), (), s32[]{:S(2)}) async-start(), calls=%async_computation.9 | async-start | bytes 5242880 | tf_op jit(solution)/shard_map/all_gather | solution.py:181
  64.2 373.3 %all-gather.16.cloned.1.call-start = ((), (), s32[]{:S(2)}) async-start(), calls=%async_computation.11 | async-start | bytes 2359296 | tf_op jit(solution)/shard_map/all_gather | solution.py:171
  64.7 491.2 %reduce-scatter.10.cloned.1.call-start = ((), (), s32[]{:S(2)}) async-start(), calls=%async_computation.14 | async-start | bytes 5242880 | tf_op jit(solution)/shard_map/reduce_scatter | solution.py:253
  121.3 8.3 copy-start.18
  121.3 8.2 copy-start.20
  142.6 37.2 %copy-start.16 = (bf16[256,1024]{1,0:T(8,128)(2,1)S(1)}, bf16[256,1024]{1,0:T(8,128)(2,1)}, u32[]{:S(2)}) copy-start(bf16[256,1024]{1,0:T(8,128)(2,1)} %all_gather.50) | copy-start | bytes 1572868
  193.0 19.7 %copy-start.5 = (bf16[2,1024,4,64]{1,3,2,0:T(8,128)(2,1)}, bf16[2,1024,4,64]{1,3,2,0:T(8,128)(2,1)S(1)}, u32[]{:S(2)}) copy-start(bf16[2,1024,4,64]{1,3,2,0:T(8,128)(2,1)S(1)} %get-tuple-element.479) | copy-start | bytes 3145732 | tf_op jit(solution)/shard_map/while
  196.4 4.7 copy-start.1
  205.6 4.6 copy-start
  265.3 24.2 %copy-start.6 = (bf16[2,1024,4,64]{1,3,2,0:T(8,128)(2,1)S(1)}, bf16[2,1024,4,64]{1,3,2,0:T(8,128)(2,1)}, u32[]{:S(2)}) copy-start(bf16[2,1024,4,64]{1,3,2,0:T(8,128)(2,1)} %copy-done.5) | copy-start | bytes 3145732 | tf_op jit(solution)/shard_map/while
  289.5 19.6 %copy-start.5 = (bf16[2,1024,4,64]{1,3,2,0:T(8,128)(2,1)}, bf16[2,1024,4,64]{1,3,2,0:T(8,128)(2,1)S(1)}, u32[]{:S(2)}) copy-start(bf16[2,1024,4,64]{1,3,2,0:T(8,128)(2,1)S(1)} %get-tuple-element.479) | copy-start | bytes 3145732 | tf_op jit(solution)/shard_map/while
  292.9 4.7 copy-start.1
  302.1 4.6 copy-start
  361.7 24.2 %copy-start.6 = (bf16[2,1024,4,64]{1,3,2,0:T(8,128)(2,1)S(1)}, bf16[2,1024,4,64]{1,3,2,0:T(8,128)(2,1)}, u32[]{:S(2)}) copy-start(bf16[2,1024,4,64]{1,3,2,0:T(8,128)(2,1)} %copy-done.5) | copy-start | bytes 3145732 | tf_op jit(solution)/shard_map/while
  389.3 9.3 %copy-start.19 = (f32[2048,16]{0,1:T(8,128)S(1)}, f32[2048,16]{0,1:T(8,128)}, u32[]{:S(2)}) copy-start(f32[2048,16]{0,1:T(8,128)} %copy-done.18) | copy-start | bytes 393220
  394.4 5.6 copy-start.21
  410.0 145.9 %reduce-scatter.12.cloned.1.call-start = ((), (), s32[]{:S(2)}) async-start(), calls=%async_computation.15 | async-start | bytes 5242880 | tf_op jit(solution)/shard_map/reduce_scatter | solution.py:256
  437.5 30.0 %copy-start.40 = (bf16[1024,1024]{1,0:T(8,128)(2,1)S(1)}, bf16[1024,1024]{1,0:T(8,128)(2,1)}, u32[]{:S(2)}) copy-start(bf16[1024,1024]{1,0:T(8,128)(2,1)} %all-gather.14.cloned.1.call-done) | copy-start | bytes 6291460
  473.8 130.7 %reduce-scatter.8.cloned.1.call-start = ((), (), s32[]{:S(2)}) async-start(), calls=%async_computation.12 | async-start | bytes 5242880 | tf_op jit(solution)/shard_map/reduce_scatter | solution.py:205
  476.7 12.3 %copy-start.39 = (bf16[1024,1024]{1,0:T(8,128)(2,1)S(1)}, bf16[1024,1024]{1,0:T(8,128)(2,1)}, u32[]{:S(2)}) copy-start(bf16[1024,1024]{1,0:T(8,128)(2,1)} %all-gather.16.cloned.1.call-done) | copy-start | bytes 6291460
  489.0 6.4 copy-start.17
  498.7 133.2 %reduce-scatter.16.cloned.1.call-start = ((), (), s32[]{:S(2)}) async-start(), calls=%async_computation.17 | async-start | bytes 1179648 | tf_op jit(solution)/shard_map/reduce_scatter | solution.py:244
  503.3 206.1 %reduce-scatter.14.cloned.1.call-start = ((), (), s32[]{:S(2)}) async-start(), calls=%async_computation.16 | async-start | bytes 3538944 | tf_op jit(solution)/shard_map/reduce_scatter | solution.py:242
  511.7 288.8 %reduce-scatter.20.cloned.1.call-start = ((), (), s32[]{:S(2)}) async-start(), calls=%async_computation.19 | async-start | bytes 4718592 | tf_op jit(solution)/shard_map/reduce_scatter | solution.py:245
  522.1 370.9 %reduce-scatter.18.cloned.1.call-start = ((), (), s32[]{:S(2)}) async-start(), calls=%async_computation.18 | async-start | bytes 4718592 | tf_op jit(solution)/shard_map/reduce_scatter | solution.py:243
  532.7 23.3 %copy-start.7 = (bf16[512,1024]{1,0:T(8,128)(2,1)S(1)}, bf16[512,1024]{1,0:T(8,128)(2,1)}, u32[]{:S(2)}) copy-start(bf16[512,1024]{1,0:T(8,128)(2,1)} %param.19) | copy-start | bytes 3145732
  532.7 23.3 %copy-start.23 = (f32[512]{0:T(512)S(1)}, f32[512]{0:T(512)}, u32[]{:S(2)}) copy-start(f32[512]{0:T(512)} %copy-done.22) | copy-start | bytes 6148
  532.7 23.3 %copy-start.25 = (f32[1024]{0:T(1024)S(1)}, f32[1024]{0:T(1024)}, u32[]{:S(2)}) copy-start(f32[1024]{0:T(1024)} %copy-done.24) | copy-start | bytes 12292
  532.7 23.3 %copy-start.27 = (f32[1024]{0:T(1024)S(1)}, f32[1024]{0:T(1024)}, u32[]{:S(2)}) copy-start(f32[1024]{0:T(1024)} %copy-done.26) | copy-start | bytes 12292
  532.7 25.9 %copy-start.35 = (f32[512]{0:T(512)S(1)}, f32[512]{0:T(512)}, u32[]{:S(2)}) copy-start(f32[512]{0:T(512)} %copy-done.34) | copy-start | bytes 6148
  532.7 25.9 %copy-start.30 = (f32[512]{0:T(512)S(1)}, f32[512]{0:T(512)}, u32[]{:S(2)}) copy-start(f32[512]{0:T(512)} %copy-done.29) | copy-start | bytes 6148
  532.7 29.3 %copy-start.12 = (bf16[512,1024]{1,0:T(8,128)(2,1)S(1)}, bf16[512,1024]{1,0:T(8,128)(2,1)}, u32[]{:S(2)}) copy-start(bf16[512,1024]{1,0:T(8,128)(2,1)} %param.21) | copy-start | bytes 3145732
  532.7 29.3 %copy-start.33 = (f32[512]{0:T(512)S(1)}, f32[512]{0:T(512)}, u32[]{:S(2)}) copy-start(f32[512]{0:T(512)} %copy-done.32) | copy-start | bytes 6148
  555.9 6.1 copy-start.9
  555.9 6.1 copy-start.10
  602.2 291.3 %copy-start.45 = (f32[32]{0:T(128)}, f32[32]{0:T(128)S(1)}, u32[]{:S(2)}) copy-start(f32[32]{0:T(128)S(1)} %dynamic-slice.7) | copy-start | bytes 388
  (20 other events, 39.0 us)
Sparse Core Ops, SparseCore 0:
  10.2 47.2 all-gather.9
  61.1 34.3 all-gather.7
  97.0 34.4 all-gather.17
  133.6 49.2 all-gather.13
  184.9 32.9 all-gather.11
  219.9 49.2 all-gather.15
  410.1 41.0 reduce-scatter.9
  474.0 43.1 reduce-scatter.11
  519.7 44.4 reduce-scatter.7
  568.4 63.4 reduce-scatter.15
  636.1 73.1 reduce-scatter.13
  713.4 87.0 reduce-scatter.19
  805.1 87.8 reduce-scatter.17
where the time goes:
time: 914 us; the launch traced here: 901 us
  waiting for transfers between devices  288 us (32%)
  matrix products  186 us (20%)
  blocking collectives  171 us (19%)
  local copies, waits for them, and re-layouts  168 us (18%)
  other arithmetic  68.2 us (7%)
  between operations  17.2 us (2%)
    unnamed x4, blocking collectives  121 us
    dynamic_update_slice x12, local copies, waits for them, and re-layouts, local(): lax.map(attend_back, (shaped(query), shaped(keys), shaped(values), labels...  115 us
    reduce_scatter x1, waiting for transfers between devices, local(): lax.psum_scatter(expand_grad, 'fsdp', scatter_dimension=0, tiled=True)  92.5 us
    reduce_scatter x1, waiting for transfers between devices, local(): lax.psum_scatter(shrink_grad, 'fsdp', scatter_dimension=0, tiled=True)  91.2 us
    reduce_scatter x1, waiting for transfers between devices, local(): lax.psum_scatter(project_grad, 'fsdp', scatter_dimension=0, tiled=True)  77.4 us
    dot_general x4, matrix products, contract_columns(): lax.dot_general(left, right, (((1,), (1,)), ((), ())), preferred_element_...  44.1 us
    all_gather x1, blocking collectives, local(): lax.all_gather(dense_weight, 'fsdp', axis=0, tiled=True)  33.6 us
    dot_general x4, matrix products, contract_rows(): lax.dot_general(left, right, (((0,), (0,)), ((), ())), preferred_element_...  33.4 us
  transfers between devices with their start and end apart: 13, of which 4 were waited for; matrix products, arithmetic and copies ran while one was open for 46% of the time, Pallas kernels for 0%

commit v1 on v0

--- a/solution.py
+++ b/solution.py
@@ -10,6 +10,25 @@
 SEQ_LEN = 1024
 EPS = 1e-05
 NEGATIVE = -1e30
+
+
+def gather_around(array, axis, dim):
+    size, here, rows = (lax.axis_size(axis), lax.axis_index(axis), array.shape[dim])
+    right = [(i, (i + 1) % size) for i in range(size)]
+    backward = [(i, (i - 1) % size) for i in range(size)]
+    out = jnp.zeros((*array.shape[:dim], size * rows, *array.shape[dim + 1 :]), array.dtype)
+    out = lax.dynamic_update_slice_in_dim(out, array, here * rows, axis=dim)
+    from_left = from_right = array
+    halfway = size // 2
+    for step in range(1, halfway + 1):
+        from_left = lax.ppermute(from_left, axis, right)
+        out = lax.dynamic_update_slice_in_dim(out, from_left, (here - step) % size * rows, axis=dim)
+        if step < size - halfway:
+            from_right = lax.ppermute(from_right, axis, backward)
+            out = lax.dynamic_update_slice_in_dim(
+                out, from_right, (here + step) % size * rows, axis=dim
+            )
+    return out
 
 
 def layer_norm(values, gain, shift):
@@ -167,7 +186,7 @@
     gathered = (
         lax.all_gather(project_weight, "fsdp", axis=0, tiled=True),
         lax.all_gather(expand_weight, "fsdp", axis=0, tiled=True),
-        lax.all_gather(dense_weight, "fsdp", axis=0, tiled=True),
+        gather_around(dense_weight, "fsdp", 0),
         lax.all_gather(shrink_weight, "fsdp", axis=0, tiled=True),
         lax.all_gather(project_bias, "fsdp", axis=0, tiled=True),
         lax.all_gather(expand_bias, "fsdp", axis=0, tiled=True),

time: 914 us -> 903 us (0.988)
  blocking collectives: 171 us -> 135 us
  starting transfers between devices: 0.99 us -> 15.4 us
    all_gather x1 -> x0, blocking collectives: 33.6 us -> none  [local(): lax.all_gather(dense_weight, 'fsdp', axis=0, tiled=True)]
    ppermute x0 -> x7, starting transfers between devices: none -> 14.4 us  [the longest x3 10.9 us: gather_around(): from_right = lax.ppermute(from_right, axis, backward)]
  transfers between devices with their start and end apart: 13 -> 20, of which waited for: 4 -> 7; matrix products, arithmetic and copies ran while one was open for 46% -> 47% of each run, Pallas kernels for 0% -> 0%
where the time goes in v1:
time: 903 us; the launch traced here: 889 us
  waiting for transfers between devices  295 us (33%)
  matrix products  186 us (21%)
  local copies, waits for them, and re-layouts  172 us (19%)
  blocking collectives  135 us (15%)
  other arithmetic  66.4 us (7%)
  between operations  17.4 us (2%)
  starting transfers between devices  15.4 us (2%)
    unnamed x4, blocking collectives  119 us
    dynamic_update_slice x12, local copies, waits for them, and re-layouts, local(): lax.map(attend_back, (shaped(query), shaped(keys), shaped(values), labels...  115 us
    reduce_scatter x1, waiting for transfers between devices, local(): lax.psum_scatter(expand_grad, 'fsdp', scatter_dimension=0, tiled=True)  92.3 us
    reduce_scatter x1, waiting for transfers between devices, local(): lax.psum_scatter(shrink_grad, 'fsdp', scatter_dimension=0, tiled=True)  91.1 us
    reduce_scatter x1, waiting for transfers between devices, local(): lax.psum_scatter(project_grad, 'fsdp', scatter_dimension=0, tiled=True)  77.5 us
    dot_general x4, matrix products, contract_columns(): lax.dot_general(left, right, (((1,), (1,)), ((), ())), preferred_element_...  43.2 us
    dot_general x4, matrix products, contract_rows(): lax.dot_general(left, right, (((0,), (0,)), ((), ())), preferred_element_...  33.5 us
    reduce_scatter x1, waiting for transfers between devices, local(): lax.psum_scatter(dense_grad, 'fsdp', scatter_dimension=0, tiled=True)  24.4 us
  transfers between devices with their start and end apart: 20, of which 7 were waited for; matrix products, arithmetic and copies ran while one was open for 47% of the time, Pallas kernels for 0%

profile of v1, /device:TPU:0, one launch (start us, length us, event | category | flops | bytes accessed | tf_op | source)
XLA Modules:
  0.0 888.8 jit_solution(11332679227281956693)
XLA Ops:
  11.4 42.8 %all-reduce.15 = (f32[1024]{0:T(1024)S(1)}, f32[1024]{0:T(1024)S(1)}, f32[1024]{0:T(1024)S(1)}, f32[1024]{0:T(1024)S(1)}) all-reduce(f32[1024]{0:T(1024)S(1)} %dynamic-update-slice.4, f32[1024]{0:T(1024)S(1)} %dynamic-update-slice.3, f32[1024]{0:T(1024)S(1)} %dynamic-update-slice.1, ...), channel_id=1, replica_groups=mesh['fsdp'=8,'tensor'=4] {'fsdp','tensor'}, use_global_device_ids=true, to_apply=%add.4 | all-reduce | flops 4096 | bytes 32768
  70.4 18.1 %all-reduce.2 = bf16[768]{0:T(1024)(128)(2,1)S(1)} all-reduce(bf16[768]{0:T(1024)(128)(2,1)S(1)} %dynamic-update-slice.2), channel_id=1, replica_groups=mesh['fsdp'=8,'tensor'=4] {'fsdp'}, use_global_device_ids=true, to_apply=%add.2 | all-reduce | flops 768 | bytes 3072
  91.4 3.7 collective-permute-start.3
  97.7 4.7 collective-permute-start.5
  106.1 5.7 collective-permute-done.6
  112.4 5.8 convolution_add_fusion.1
  133.6 37.7 %while.26 = (s32[]{:T(128)}, bf16[2,1024,4,64]{1,3,2,0:T(8,128)(2,1)}, f32[2,4,1024]{2,1,0:T(4,128)S(1)}, bf16[2,1024,4,64]{1,3,2,0:T(8,128)(2,1)}, s32[2,1024]{...) while((s32[]{:T(128)}, ...), condition=%wide.region_7.8_spmd, body=%wide.region_2.7_spmd.sunk | while | flops 1131677184 | bytes 67310776 | solution.py:217
  144.2 3.6 fusion.212
  147.9 3.7 fusion.209
  162.9 3.6 fusion.212
  166.5 3.7 fusion.209
  176.8 4.1 copy.57
  180.9 193.2 %while.27 = (s32[]{:T(128)}, f32[2,1024,4,64]{1,0,3,2:T(2,128)}, f32[2,1024,4,64]{1,0,3,2:T(2,128)}, bf16[2,1024,4,64]{1,0,3,2:T(2,128)(2,1)}, bf16[2,1024,4,64]...) while((s32[]{:T(128)}, f32[2,1024,4,64]{1,0,3,2:T(2,128)}, ...), condition=%wide.region_12.13_spmd, body=%wide.region_9.12_spmd.sunk | while | flops 2755130880 | bytes 284876160 | solution.py:249
  184.5 4.6 multiply_reduce_fusion.5
  193.6 4.6 multiply_reduce_fusion.4
  203.8 18.7 %dynamic_update_slice.68 = f32[2,1024,4,64]{1,0,3,2:T(2,128)} dynamic-update-slice(f32[2,1024,4,64]{1,0,3,2:T(2,128)} %get-tuple-element.462, f32[1,1024,4,64]{1,0,3,2:T(1,128)S(1)} %copy.97, s32[]{:T(128)} %get-tuple-element.460, s32[]{:T(128)} %constant.166.clone.1..sunk.1, s32[]{:T(128)} %constant.166.clone.1..sunk.1, s32[]{:T(128)} %constant.166.clone.1..sunk.1) | dynamic-update-slice | bytes 2097156 | tf_op jit(solution)/shard_map/while/body/jit(dynamic_update_index_in_dim)/dynamic_update_slice | solution.py:249
  222.5 3.7 fusion.230
  228.8 18.7 %dynamic_update_slice.67 = f32[2,1024,4,64]{1,0,3,2:T(2,128)} dynamic-update-slice(f32[2,1024,4,64]{1,0,3,2:T(2,128)} %get-tuple-element.461, f32[1,1024,4,64]{1,0,3,2:T(1,128)S(1)} %copy.96, s32[]{:T(128)} %get-tuple-element.460, s32[]{:T(128)} %constant.166.clone.1..sunk.1, s32[]{:T(128)} %constant.166.clone.1..sunk.1, s32[]{:T(128)} %constant.166.clone.1..sunk.1) | dynamic-update-slice | bytes 2097156 | tf_op jit(solution)/shard_map/while/body/jit(dynamic_update_index_in_dim)/dynamic_update_slice | solution.py:249
  247.4 5.7 fusion.233
  253.2 5.9 fusion.234
  260.0 17.4 %dynamic_update_slice.69 = bf16[2,1024,4,64]{1,0,3,2:T(2,128)(2,1)} dynamic-update-slice(bf16[2,1024,4,64]{1,0,3,2:T(2,128)(2,1)} %get-tuple-element.463, bf16[1,1024,4,64]{1,0,3,2:T(2,128)(2,1)S(1)} %copy.98, s32[]{:T(128)} %get-tuple-element.460, s32[]{:T(128)} %constant.166.clone.1..sunk.1, s32[]{:T(128)} %constant.166.clone.1..sunk.1, s32[]{:T(128)} %constant.166.clone.1..sunk.1) | dynamic-update-slice | bytes 1048580 | tf_op jit(solution)/shard_map/while/body/jit(dynamic_update_index_in_dim)/dynamic_update_slice | solution.py:249
  280.8 4.6 multiply_reduce_fusion.5
  290.0 4.6 multiply_reduce_fusion.4
  300.2 18.7 %dynamic_update_slice.68 = f32[2,1024,4,64]{1,0,3,2:T(2,128)} dynamic-update-slice(f32[2,1024,4,64]{1,0,3,2:T(2,128)} %get-tuple-element.462, f32[1,1024,4,64]{1,0,3,2:T(1,128)S(1)} %copy.97, s32[]{:T(128)} %get-tuple-element.460, s32[]{:T(128)} %constant.166.clone.1..sunk.1, s32[]{:T(128)} %constant.166.clone.1..sunk.1, s32[]{:T(128)} %constant.166.clone.1..sunk.1) | dynamic-update-slice | bytes 2097156 | tf_op jit(solution)/shard_map/while/body/jit(dynamic_update_index_in_dim)/dynamic_update_slice | solution.py:249
  318.8 3.7 fusion.230
  325.1 18.7 %dynamic_update_slice.67 = f32[2,1024,4,64]{1,0,3,2:T(2,128)} dynamic-update-slice(f32[2,1024,4,64]{1,0,3,2:T(2,128)} %get-tuple-element.461, f32[1,1024,4,64]{1,0,3,2:T(1,128)S(1)} %copy.96, s32[]{:T(128)} %get-tuple-element.460, s32[]{:T(128)} %constant.166.clone.1..sunk.1, s32[]{:T(128)} %constant.166.clone.1..sunk.1, s32[]{:T(128)} %constant.166.clone.1..sunk.1) | dynamic-update-slice | bytes 2097156 | tf_op jit(solution)/shard_map/while/body/jit(dynamic_update_index_in_dim)/dynamic_update_slice | solution.py:249
  343.8 5.7 fusion.233
  349.5 5.9 fusion.234
  356.3 17.4 %dynamic_update_slice.69 = bf16[2,1024,4,64]{1,0,3,2:T(2,128)(2,1)} dynamic-update-slice(bf16[2,1024,4,64]{1,0,3,2:T(2,128)(2,1)} %get-tuple-element.463, bf16[1,1024,4,64]{1,0,3,2:T(2,128)(2,1)S(1)} %copy.98, s32[]{:T(128)} %get-tuple-element.460, s32[]{:T(128)} %constant.166.clone.1..sunk.1, s32[]{:T(128)} %constant.166.clone.1..sunk.1, s32[]{:T(128)} %constant.166.clone.1..sunk.1) | dynamic-update-slice | bytes 1048580 | tf_op jit(solution)/shard_map/while/body/jit(dynamic_update_index_in_dim)/dynamic_update_slice | solution.py:249
  377.2 4.1 reshape.509
  392.6 5.3 convolution_convert_fusion
  398.5 16.1 %all-gather = bf16[8,1,128]{2,1,0:T(2,128)(2,1)S(1)} all-gather(bf16[1,1,128]{2,1,0:T(2,128)(2,1)S(1)} %bitcast.260), channel_id=1, replica_groups=mesh['fsdp'=8,'tensor'=4] {'fsdp'}, dimensions={0}, use_global_device_ids=true | all-gather | bytes 2304 | tf_op jit(solution)/shard_map/all_gather | solution.py:192
  414.7 10.7 %fusion.139 = f32[2048,1024]{1,0:T(8,128)} fusion(bf16[2048,1024]{1,0:T(8,128)(2,1)} %all-gather.12.cloned.1.call-done, bf16[1024,1024]{1,0:T(8,128)(2,1)} %all-gather.14.cloned.1.call-done), kind=kOutput, calls=%fused_computation.253 | convolution fusion | flops 4294967296 | bytes 14680064 | tf_op jit(solution)/shard_map/dot_general | solution.py:219
  425.4 27.9 %convert_reduce_fusion = (f32[1024]{0:T(1024)S(1)}, bf16[2048,1024]{1,0:T(8,128)(2,1)S(1)}, f32[2048,1024]{1,0:T(8,128)}) fusion(f32[2048,1024]{1,0:T(8,128)} %fusion.139, f32[1024]{0:T(1024)S(1)} %bitcast.258, bf16[2048,1024]{1,0:T(8,128)(2,1)} %all-gather.18.cloned.1.call-done, bf16[1024,1024]{1,0:T(8,128)(2,1)} %all-gather.16.cloned.1.call-done), kind=kOutput, calls=%fused_computation.132 | convolution fusion | flops 4452252672 | bytes 27271168 | tf_op jit(solution)/shard_map/dot_general | solution.py:151
  455.3 6.4 convolution_convert_fusion.1
  464.3 12.1 %multiply_convert_fusion.2 = bf16[2048,1024]{1,0:T(8,128)(2,1)} fusion(f32[2048,1024]{1,0:T(8,128)} %get-tuple-element.214, f32[2048,1024]{1,0:T(8,128)} %fusion.139, f32[1024]{0:T(1024)S(1)} %bitcast.259), kind=kLoop, calls=%fused_computation.135 | loop fusion | flops 8388608 | bytes 20975616 | tf_op jit(solution)/shard_map/convert_element_type | solution.py:222
  476.4 6.3 fusion.140
  482.7 4.4 add_convert_fusion.1
  487.2 4.5 fusion.142
  491.7 8.4 fusion.141
  500.4 10.1 %fusion.144 = f32[1024,1024]{1,0:T(8,128)} fusion(bf16[2048,1024]{1,0:T(8,128)(2,1)} %multiply_convert_fusion.2, bf16[2048,1024]{1,0:T(8,128)(2,1)} %all-gather.18.cloned.1.call-done), kind=kOutput, calls=%fused_computation.258 | convolution fusion | flops 4294967296 | bytes 12582912 | tf_op jit(solution)/shard_map/dot_general | solution.py:145
  510.6 10.6 %fusion.143 = f32[1024,1024]{1,0:T(8,128)} fusion(bf16[2048,1024]{1,0:T(8,128)(2,1)} %all-gather.12.cloned.1.call-done, bf16[2048,1024]{1,0:T(8,128)(2,1)} %copy-done.47), kind=kOutput, calls=%fused_computation.257 | convolution fusion | flops 4294967296 | bytes 12582912 | tf_op jit(solution)/shard_map/dot_general | solution.py:145
  523.3 19.9 %all-reduce.16 = (f32[768]{0:T(1024)S(1)}, f32[1024]{0:T(1024)S(1)}) all-reduce(f32[768]{0:T(1024)S(1)} %reduce_sum.174, f32[1024]{0:T(1024)S(1)} %get-tuple-element.212), channel_id=10, replica_groups=mesh['fsdp'=8,'tensor'=4] {'fsdp'}, use_global_device_ids=true, to_apply=%region_29.30.clone | all-reduce | flops 1792 | bytes 14336
  553.1 37.7 %all-reduce.14 = (f32[1024]{0:T(1024)S(1)}, f32[1024]{0:T(1024)S(1)}, f32[1024]{0:T(1024)S(1)}, f32[1024]{0:T(1024)S(1)}, f32[1024]{0:T(1024)S(1)}, /*index=5*/f32[1024]{0:T(1024)S(1)}, f32[1024]{0:T(1024)S(1)}) all-reduce(f32[1024]{0:T(1024)S(1)} %dynamic-update-slice.6, ...), channel_id=1, replica_groups=mesh['fsdp'=8,'tensor'=4] {'fsdp','tensor'}, use_global_device_ids=true, to_apply=%add.6 | all-reduce | flops 7168 | bytes 57344
  595.9 24.4 %reduce-scatter.16.cloned.1.call-done = f32[32,1024]{1,0:T(8,128)} async-done(((f32[256,1024]{1,0:T(8,128)}), f32[32,1024]{1,0:T(8,128)}) %reduce-scatter.16.cloned.1.call-update) | async-done | bytes 131088 | tf_op jit(solution)/shard_map/reduce_scatter | solution.py:263
  620.3 77.5 %reduce-scatter.14.cloned.1.call-done = f32[128,768]{1,0:T(8,128)} async-done(((f32[1024,768]{1,0:T(8,128)}), f32[128,768]{1,0:T(8,128)}) %reduce-scatter.14.cloned.1.call-update) | async-done | bytes 393232 | tf_op jit(solution)/shard_map/reduce_scatter | solution.py:261
  697.9 91.1 %reduce-scatter.20.cloned.1.call-done = f32[128,1024]{1,0:T(8,128)} async-done(((f32[1024,1024]{1,0:T(8,128)}), f32[128,1024]{1,0:T(8,128)}) %reduce-scatter.20.cloned.1.call-update) | async-done | bytes 524304 | tf_op jit(solution)/shard_map/reduce_scatter | solution.py:264
  788.9 92.3 %reduce-scatter.18.cloned.1.call-done = f32[128,1024]{1,0:T(8,128)} async-done(((f32[1024,1024]{1,0:T(8,128)}), f32[128,1024]{1,0:T(8,128)}) %reduce-scatter.18.cloned.1.call-update) | async-done | bytes 524304 | tf_op jit(solution)/shard_map/reduce_scatter | solution.py:262
  (319 shorter events, 141.6 us)
Async XLA Ops:
  7.2 54.0 %copy-start.37 = (s32[2048]{0:T(1024)S(1)}, s32[2048]{0:T(1024)}, u32[]{:S(2)}) copy-start(s32[2048]{0:T(1024)} %param.20) | copy-start | bytes 24580
  7.2 54.1 %copy-start.11 = (bf16[512,1024]{1,0:T(8,128)(2,1)S(1)}, bf16[512,1024]{1,0:T(8,128)(2,1)}, u32[]{:S(2)}) copy-start(bf16[512,1024]{1,0:T(8,128)(2,1)} %param.21) | copy-start | bytes 3145732
  7.2 105.2 %all-gather.10.cloned.1.call-start = ((), (), s32[]{:S(2)}) async-start(), calls=%async_computation.8 | async-start | bytes 1769472 | tf_op jit(solution)/shard_map/all_gather | solution.py:187
  7.9 104.5 %all-gather.8.cloned.1.call-start = ((), (), s32[]{:S(2)}) async-start(), calls=%async_computation.7 | async-start | bytes 5242880 | tf_op jit(solution)/shard_map/all_gather | solution.py:199
  54.2 8.3 copy-start.25
  54.2 8.3 copy-start.27
  57.3 6.4 copy-start.30
  57.9 10.9 %copy-start.38 = (u32[32]{0:T(128)S(1)}, u32[32]{0:T(128)}, u32[]{:S(2)}) copy-start(u32[32]{0:T(128)} %constant.231) | copy-start | bytes 388
  57.9 12.2 %copy-start.43 = (bf16[96]{0:T(256)(128)(2,1)S(1)}, bf16[96]{0:T(256)(128)(2,1)}, u32[]{:S(2)}) copy-start(bf16[96]{0:T(256)(128)(2,1)} %param.27) | copy-start | bytes 580
  61.1 110.2 %all-gather.18.cloned.1.call-start = ((), (), s32[]{:S(2)}) async-start(), calls=%async_computation.13 | async-start | bytes 5242880 | tf_op jit(solution)/shard_map/all_gather | solution.py:236
  61.3 27.2 %copy-start.33 = (f32[512]{0:T(512)}, f32[512]{0:T(512)S(1)}, u32[]{:S(2)}) copy-start(f32[512]{0:T(512)S(1)} %fusion.131) | copy-start | bytes 6148
  62.5 352.1 %all-gather.14.cloned.1.call-start = ((), (), s32[]{:S(2)}) async-start(), calls=%async_computation.10 | async-start | bytes 2359296 | tf_op jit(solution)/shard_map/all_gather | solution.py:188
  63.1 351.5 %all-gather.12.cloned.1.call-start = ((), (), s32[]{:S(2)}) async-start(), calls=%async_computation.9 | async-start | bytes 5242880 | tf_op jit(solution)/shard_map/all_gather | solution.py:200
  63.7 361.6 %all-gather.16.cloned.1.call-start = ((), (), s32[]{:S(2)}) async-start(), calls=%async_computation.11 | async-start | bytes 2359296 | tf_op jit(solution)/shard_map/all_gather | solution.py:190
  63.8 26.6 %collective-permute-start = (bf16[32,1024]{1,0:T(8,128)(2,1)S(1)}, bf16[32,1024]{1,0:T(8,128)(2,1)S(1)}, u32[]{:S(2)}, u32[]{:S(2)}) collective-permute-start(bf16[32,1024]{1,0:T(8,128)(2,1)S(1)} %copy-done.29), channel_id=1, source_target_pairs={{0,4},{4,8},{8,12},{12,16},{16,20},{20,24},{24,28},{28,0},{1,5},{5... | collective-permute-start | bytes 196616 | tf_op jit(solution)/shard_map/ppermute | solution.py:24
  66.1 25.3 %collective-permute-start.1 = (bf16[32,1024]{1,0:T(8,128)(2,1)S(1)}, bf16[32,1024]{1,0:T(8,128)(2,1)S(1)}, u32[]{:S(2)}, u32[]{:S(2)}) collective-permute-start(bf16[32,1024]{1,0:T(8,128)(2,1)S(1)} %copy-done.29), channel_id=1, source_target_pairs={{0,28},{4,0},{8,4},{12,8},{16,12},{20,16},{24,20},{28,24},{1,29},{... | collective-permute-start | bytes 196616 | tf_op jit(solution)/shard_map/ppermute | solution.py:27
  68.6 475.8 %reduce-scatter.10.cloned.1.call-start = ((), (), s32[]{:S(2)}) async-start(), calls=%async_computation.14 | async-start | bytes 5242880 | tf_op jit(solution)/shard_map/reduce_scatter | solution.py:272
  88.8 31.7 %copy-start.16 = (f32[2048,16]{0,1:T(8,128)}, f32[2048,16]{0,1:T(8,128)S(1)}, u32[]{:S(2)}) copy-start(f32[2048,16]{0,1:T(8,128)S(1)} %get-tuple-element.268) | copy-start | bytes 393220
  88.8 31.7 %copy-start.18 = (f32[2048,16]{0,1:T(8,128)}, f32[2048,16]{0,1:T(8,128)S(1)}, u32[]{:S(2)}) copy-start(f32[2048,16]{0,1:T(8,128)S(1)} %get-tuple-element.267) | copy-start | bytes 393220
  90.4 7.3 collective-permute-start.2
  91.4 6.2 collective-permute-start.3
  97.6 7.0 collective-permute-start.4
  97.7 7.8 collective-permute-start.5
  104.6 7.2 collective-permute-start.6
  181.0 19.6 %copy-start.5 = (bf16[2,1024,4,64]{1,3,2,0:T(8,128)(2,1)}, bf16[2,1024,4,64]{1,3,2,0:T(8,128)(2,1)S(1)}, u32[]{:S(2)}) copy-start(bf16[2,1024,4,64]{1,3,2,0:T(8,128)(2,1)S(1)} %get-tuple-element.479) | copy-start | bytes 3145732 | tf_op jit(solution)/shard_map/while
  253.2 24.2 %copy-start.6 = (bf16[2,1024,4,64]{1,3,2,0:T(8,128)(2,1)S(1)}, bf16[2,1024,4,64]{1,3,2,0:T(8,128)(2,1)}, u32[]{:S(2)}) copy-start(bf16[2,1024,4,64]{1,3,2,0:T(8,128)(2,1)} %copy-done.5) | copy-start | bytes 3145732 | tf_op jit(solution)/shard_map/while
  277.4 19.6 %copy-start.5 = (bf16[2,1024,4,64]{1,3,2,0:T(8,128)(2,1)}, bf16[2,1024,4,64]{1,3,2,0:T(8,128)(2,1)S(1)}, u32[]{:S(2)}) copy-start(bf16[2,1024,4,64]{1,3,2,0:T(8,128)(2,1)S(1)} %get-tuple-element.479) | copy-start | bytes 3145732 | tf_op jit(solution)/shard_map/while
  349.5 24.2 %copy-start.6 = (bf16[2,1024,4,64]{1,3,2,0:T(8,128)(2,1)S(1)}, bf16[2,1024,4,64]{1,3,2,0:T(8,128)(2,1)}, u32[]{:S(2)}) copy-start(bf16[2,1024,4,64]{1,3,2,0:T(8,128)(2,1)} %copy-done.5) | copy-start | bytes 3145732 | tf_op jit(solution)/shard_map/while
  377.1 9.3 %copy-start.17 = (f32[2048,16]{0,1:T(8,128)S(1)}, f32[2048,16]{0,1:T(8,128)}, u32[]{:S(2)}) copy-start(f32[2048,16]{0,1:T(8,128)} %copy-done.16) | copy-start | bytes 393220
  397.9 146.6 %reduce-scatter.12.cloned.1.call-start = ((), (), s32[]{:S(2)}) async-start(), calls=%async_computation.15 | async-start | bytes 5242880 | tf_op jit(solution)/shard_map/reduce_scatter | solution.py:275
  425.4 29.9 %copy-start.40 = (bf16[1024,1024]{1,0:T(8,128)(2,1)S(1)}, bf16[1024,1024]{1,0:T(8,128)(2,1)}, u32[]{:S(2)}) copy-start(bf16[1024,1024]{1,0:T(8,128)(2,1)} %all-gather.14.cloned.1.call-done) | copy-start | bytes 6291460
  461.7 131.5 %reduce-scatter.8.cloned.1.call-start = ((), (), s32[]{:S(2)}) async-start(), calls=%async_computation.12 | async-start | bytes 5242880 | tf_op jit(solution)/shard_map/reduce_scatter | solution.py:224
  464.3 12.2 %copy-start.41 = (bf16[1024,1024]{1,0:T(8,128)(2,1)S(1)}, bf16[1024,1024]{1,0:T(8,128)(2,1)}, u32[]{:S(2)}) copy-start(bf16[1024,1024]{1,0:T(8,128)(2,1)} %all-gather.16.cloned.1.call-done) | copy-start | bytes 6291460
  487.1 133.2 %reduce-scatter.16.cloned.1.call-start = ((), (), s32[]{:S(2)}) async-start(), calls=%async_computation.17 | async-start | bytes 1179648 | tf_op jit(solution)/shard_map/reduce_scatter | solution.py:263
  491.7 206.2 %reduce-scatter.14.cloned.1.call-start = ((), (), s32[]{:S(2)}) async-start(), calls=%async_computation.16 | async-start | bytes 3538944 | tf_op jit(solution)/shard_map/reduce_scatter | solution.py:261
  500.1 288.8 %reduce-scatter.20.cloned.1.call-start = ((), (), s32[]{:S(2)}) async-start(), calls=%async_computation.19 | async-start | bytes 4718592 | tf_op jit(solution)/shard_map/reduce_scatter | solution.py:264
  510.5 370.7 %reduce-scatter.18.cloned.1.call-start = ((), (), s32[]{:S(2)}) async-start(), calls=%async_computation.18 | async-start | bytes 4718592 | tf_op jit(solution)/shard_map/reduce_scatter | solution.py:262
  521.2 23.2 %copy-start.7 = (bf16[512,1024]{1,0:T(8,128)(2,1)S(1)}, bf16[512,1024]{1,0:T(8,128)(2,1)}, u32[]{:S(2)}) copy-start(bf16[512,1024]{1,0:T(8,128)(2,1)} %param.19) | copy-start | bytes 3145732
  521.2 23.2 %copy-start.24 = (f32[512]{0:T(512)S(1)}, f32[512]{0:T(512)}, u32[]{:S(2)}) copy-start(f32[512]{0:T(512)} %copy-done.23) | copy-start | bytes 6148
  521.2 23.2 %copy-start.26 = (f32[1024]{0:T(1024)S(1)}, f32[1024]{0:T(1024)}, u32[]{:S(2)}) copy-start(f32[1024]{0:T(1024)} %copy-done.25) | copy-start | bytes 12292
  521.2 23.2 %copy-start.28 = (f32[1024]{0:T(1024)S(1)}, f32[1024]{0:T(1024)}, u32[]{:S(2)}) copy-start(f32[1024]{0:T(1024)} %copy-done.27) | copy-start | bytes 12292
  521.2 25.9 %copy-start.36 = (f32[512]{0:T(512)S(1)}, f32[512]{0:T(512)}, u32[]{:S(2)}) copy-start(f32[512]{0:T(512)} %copy-done.35) | copy-start | bytes 6148
  521.2 25.9 %copy-start.31 = (f32[512]{0:T(512)S(1)}, f32[512]{0:T(512)}, u32[]{:S(2)}) copy-start(f32[512]{0:T(512)} %copy-done.30) | copy-start | bytes 6148
  521.3 29.3 %copy-start.12 = (bf16[512,1024]{1,0:T(8,128)(2,1)S(1)}, bf16[512,1024]{1,0:T(8,128)(2,1)}, u32[]{:S(2)}) copy-start(bf16[512,1024]{1,0:T(8,128)(2,1)} %param.21) | copy-start | bytes 3145732
  521.3 29.3 %copy-start.34 = (f32[512]{0:T(512)S(1)}, f32[512]{0:T(512)}, u32[]{:S(2)}) copy-start(f32[512]{0:T(512)} %copy-done.33) | copy-start | bytes 6148
  544.4 6.1 copy-start.9
  544.5 6.1 copy-start.10
  590.9 290.8 %copy-start.46 = (f32[32]{0:T(128)}, f32[32]{0:T(128)S(1)}, u32[]{:S(2)}) copy-start(f32[32]{0:T(128)S(1)} %dynamic-slice.7) | copy-start | bytes 388
  (30 other events, 79.1 us)
Sparse Core Ops, SparseCore 0:
  10.2 47.2 all-gather.9
  61.3 34.1 all-gather.7
  97.0 34.4 all-gather.17
  133.5 49.4 all-gather.13
  185.0 32.9 all-gather.11
  220.0 49.5 all-gather.15
  398.0 41.4 reduce-scatter.9
  461.8 43.6 reduce-scatter.11
  508.0 44.4 reduce-scatter.7
  556.8 63.4 reduce-scatter.15
  624.5 73.3 reduce-scatter.13
  701.9 86.9 reduce-scatter.19
  793.6 87.6 reduce-scatter.17
